TPU v7x, 32 devices: a whole 2x2x4 slice. The times are simulated.
32 devices in a mesh: weight: 2 (over x), ctx: 4 (over z), tensor: 4 (over y, core).
Axes of the slice: x: 2, y: 2, z: 4, core: 2. Of those that a mesh axis runs over, the one named last changes fastest.
Arguments:
- inputs: bfloat16 [2, 1024, 1024], P('weight', 'ctx'), may hold values from -40 to 40
- w_qkv: bfloat16 [1024, 3, 1024], P('weight', None, 'tensor'), may hold values from -4 to 4
- w_out: bfloat16 [1024, 1024], P('weight', 'tensor'), may hold values from -2 to 2
- w_up: bfloat16 [1024, 4096], P('weight', 'tensor'), may hold values from -0.1875 to 0.1875
- w_down: bfloat16 [1024, 4096], P('weight', 'tensor'), may hold values from -0.09375 to 0.09375
- head_bias: float32 [2, 1024], P(None, 'tensor'), may hold values from -3 to 3
- up_bias: float32 [4096], P('tensor'), may hold values from -3 to 3
- out_biases: float32 [2, 1024], replicated, may hold values from -3 to 3
- norm_gains: float32 [2, 1024], replicated, may hold values from 0.1 to 1.9
- norm_shifts: float32 [2, 1024], replicated, may hold values from -3 to 3
- cotangent: bfloat16 [2, 1024, 1024], P('weight', 'ctx'), may hold values from -6 to 6
Outputs:
- layer_out: bfloat16 [2, 1024, 1024], P('weight', 'ctx')
- grad_input: bfloat16 [2, 1024, 1024], P('weight', 'ctx')
- grad_w_qkv: float32 [1024, 3, 1024], P(('weight', 'ctx'), None, 'tensor')
- grad_w_out: float32 [1024, 1024], P(('weight', 'ctx'), 'tensor')
- grad_w_up: float32 [1024, 4096], P(('weight', 'ctx'), 'tensor')
- grad_w_down: float32 [1024, 4096], P(('weight', 'ctx'), 'tensor')
- grad_head_bias: float32 [2, 1024], P(None, 'tensor')
- grad_up_bias: float32 [4096], P('tensor')
- grad_out_biases: float32 [2, 1024], replicated
- grad_norm_gains: float32 [2, 1024], replicated
- grad_norm_shifts: float32 [2, 1024], replicated
All inputs are finite; a program needn't handle non-finite values.
Results may differ from a plain program's by a relative error of at most 0.038.
Values may be sent and summed in bfloat16 or wider, within the bound.
No kernel may reach another device: no remote copies, remote signals or barrier semaphores. Data moves between devices by JAX's collectives and lax.ppermute only.
A program may use at most 128 MiB of HBM per device.

v0:
```python
import math
import jax
import jax.numpy as jnp
from jax import lax
from jax.sharding import PartitionSpec as P

HD = 64
norm_epsilon = 1e-05
inv_root_two = 1.0 / math.sqrt(2.0)
inv_root_tau = 1.0 / math.sqrt(2.0 * math.pi)


def layer_stats(hidden):
    mean_row = jnp.mean(hidden, axis=-1, keepdims=True)
    centred = hidden - mean_row
    inverse_spread = lax.rsqrt(jnp.mean(centred * centred, axis=-1, keepdims=True) + norm_epsilon)
    return (centred * inverse_spread, inverse_spread)


def layer_back(grad_norm, normed, inverse_spread):
    return inverse_spread * (
        grad_norm
        - jnp.mean(grad_norm, axis=-1, keepdims=True)
        - normed * jnp.mean(grad_norm * normed, axis=-1, keepdims=True)
    )


def gelu_value(pre_act):
    return 0.5 * pre_act * (1.0 + lax.erf(pre_act * inv_root_two))


def gelu_slope(pre_act):
    return (
        0.5 * (1.0 + lax.erf(pre_act * inv_root_two))
        + pre_act * jnp.exp(-0.5 * pre_act * pre_act) * inv_root_tau
    )


def heads_view(source):
    return source.reshape(source.shape[0], source.shape[1], -1, HD)


def settle(partial_value, row_work):
    return row_work(lax.psum(partial_value.astype(jnp.bfloat16), "tensor").astype(jnp.float32), 0)


def gather_keys(keys_flat, values_flat):
    return (
        lax.all_gather(keys_flat, "ctx", axis=1, tiled=True),
        lax.all_gather(values_flat, "ctx", axis=1, tiled=True),
    )


def key_blocks(state_now, query_heads, key_heads, value_heads, scale_factor):
    key_rows = key_heads.shape[1]
    block_size = math.gcd(512, key_rows)
    block_count = key_rows // block_size

    def one_block(state_in, block_index):
        acc_now, top_now, total_now = state_in
        key_part = lax.dynamic_slice_in_dim(key_heads, block_index * block_size, block_size, 1)
        value_part = lax.dynamic_slice_in_dim(value_heads, block_index * block_size, block_size, 1)
        scores = (
            jnp.einsum("bqhe,bkhe->bqhk", query_heads, key_part, preferred_element_type=jnp.float32)
            * scale_factor
        )
        top_next = jnp.maximum(top_now, jnp.max(scores, axis=-1))
        rescale = jnp.exp(top_now - top_next)
        weights = jnp.exp(scores - top_next[..., None])
        total_next = total_now * rescale + jnp.sum(weights, axis=-1)
        acc_next = acc_now * rescale[..., None] + jnp.einsum(
            "bqhk,bkhe->bqhe",
            weights.astype(jnp.bfloat16),
            value_part,
            preferred_element_type=jnp.float32,
        )
        return ((acc_next, top_next, total_next), None)

    state_out, ignored = lax.scan(one_block, state_now, jnp.arange(block_count))
    return state_out


def local(
    inputs,
    w_qkv,
    w_out,
    w_up,
    w_down,
    head_bias,
    up_bias,
    out_biases,
    norm_gains,
    norm_shifts,
    cotangent,
):
    batch, tok_rows = (inputs.shape[0], inputs.shape[1])
    head_cols = w_qkv.shape[2]
    heads_here = head_cols // HD
    scale_factor = HD ** (-0.5)
    qkv_full, out_full, up_full, down_full = (
        lax.all_gather(w_qkv, "weight", axis=0, tiled=True),
        lax.all_gather(w_out, "weight", axis=0, tiled=True),
        lax.all_gather(w_up, "weight", axis=0, tiled=True),
        lax.all_gather(w_down, "weight", axis=0, tiled=True),
    )
    projected = jnp.einsum("btd,dcf->btcf", inputs, qkv_full, preferred_element_type=jnp.float32)
    queries = (projected[:, :, 0] + head_bias[0]).astype(jnp.bfloat16)
    keys_flat = projected[:, :, 1].astype(jnp.bfloat16)
    values_flat = (projected[:, :, 2] + head_bias[1]).astype(jnp.bfloat16)
    query_heads = heads_view(queries)
    init_state = (
        jnp.zeros((batch, tok_rows, heads_here, HD), jnp.float32),
        jnp.full((batch, tok_rows, heads_here), -1e30, jnp.float32),
        jnp.zeros((batch, tok_rows, heads_here), jnp.float32),
    )
    state_end = key_blocks(
        init_state,
        query_heads,
        heads_view(lax.all_gather(keys_flat, "ctx", axis=1, tiled=True)),
        heads_view(lax.all_gather(values_flat, "ctx", axis=1, tiled=True)),
        scale_factor,
    )
    acc_sum, top_row, total_row = state_end
    log_sum = top_row + jnp.log(total_row)
    attended = (
        (acc_sum / total_row[..., None]).reshape(batch, tok_rows, head_cols).astype(jnp.bfloat16)
    )
    out_part = jnp.einsum("btf,of->bto", attended, out_full, preferred_element_type=jnp.float32)
    inputs_wide = inputs.astype(jnp.float32)

    def first_rows(summed, row_start):
        hidden = inputs_wide + summed + out_biases[0]
        return layer_stats(hidden)

    normed_one, inverse_one = settle(out_part, first_rows)
    mixed_one = normed_one * norm_gains[0] + norm_shifts[0]
    mixed_bf = mixed_one.astype(jnp.bfloat16)
    pre_act = (
        jnp.einsum("btd,df->btf", mixed_bf, up_full, preferred_element_type=jnp.float32) + up_bias
    )
    gelu_bf = gelu_value(pre_act).astype(jnp.bfloat16)
    down_part = jnp.einsum("btf,of->bto", gelu_bf, down_full, preferred_element_type=jnp.float32)

    def second_rows(summed, row_start):
        hidden = mixed_one + summed + out_biases[1]
        return layer_stats(hidden)

    normed_two, inverse_two = settle(down_part, second_rows)
    layer_out = (normed_two * norm_gains[1] + norm_shifts[1]).astype(jnp.bfloat16)
    grad_out = cotangent.astype(jnp.float32)
    grad_hidden_two = layer_back(grad_out * norm_gains[1], normed_two, inverse_two)
    gain_two = jnp.sum(grad_out * normed_two, axis=(0, 1))
    shift_two = jnp.sum(grad_out, axis=(0, 1))
    bias_down = jnp.sum(grad_hidden_two, axis=(0, 1))
    grad_two_bf = grad_hidden_two.astype(jnp.bfloat16)
    grad_down_w = jnp.einsum(
        "bto,btf->of", grad_two_bf, gelu_bf, preferred_element_type=jnp.float32
    )
    grad_pre = jnp.einsum(
        "bto,of->btf", grad_two_bf, down_full, preferred_element_type=jnp.float32
    ) * gelu_slope(pre_act)
    grad_up_b = jnp.sum(grad_pre, axis=(0, 1))
    grad_pre_bf = grad_pre.astype(jnp.bfloat16)
    grad_up_w = jnp.einsum("btd,btf->df", mixed_bf, grad_pre_bf, preferred_element_type=jnp.float32)
    mixed_part = jnp.einsum("btf,df->btd", grad_pre_bf, up_full, preferred_element_type=jnp.float32)

    def third_rows(summed, row_start):
        grad_mixed = grad_hidden_two + summed
        grad_hidden = layer_back(grad_mixed * norm_gains[0], normed_one, inverse_one)
        return (grad_hidden, grad_mixed)

    grad_hidden_one, grad_mixed_one = settle(mixed_part, third_rows)
    gain_one = jnp.sum(grad_mixed_one * normed_one, axis=(0, 1))
    shift_one = jnp.sum(grad_mixed_one, axis=(0, 1))
    bias_out = jnp.sum(grad_hidden_one, axis=(0, 1))
    grad_one_bf = grad_hidden_one.astype(jnp.bfloat16)
    grad_out_w = jnp.einsum(
        "bto,btf->of", grad_one_bf, attended, preferred_element_type=jnp.float32
    )
    grad_attended = jnp.einsum(
        "bto,of->btf", grad_one_bf, out_full, preferred_element_type=jnp.float32
    ).astype(jnp.bfloat16)
    grad_attended_heads = heads_view(grad_attended)
    row_delta = jnp.sum(
        grad_attended_heads.astype(jnp.float32) * heads_view(attended).astype(jnp.float32), axis=-1
    )
    keys_all, values_all = gather_keys(keys_flat, values_flat)
    key_heads = heads_view(keys_all)
    value_heads = heads_view(values_all)
    key_rows = key_heads.shape[1]
    block_size = math.gcd(512, key_rows)
    block_count = key_rows // block_size

    def back_block(state_in, block_index):
        grad_query, grad_keys, grad_values = state_in
        offset = block_index * block_size
        key_part = lax.dynamic_slice_in_dim(key_heads, offset, block_size, 1)
        value_part = lax.dynamic_slice_in_dim(value_heads, offset, block_size, 1)
        scores = (
            jnp.einsum("bqhe,bkhe->bqhk", query_heads, key_part, preferred_element_type=jnp.float32)
            * scale_factor
        )
        weights = jnp.exp(scores - log_sum[..., None])
        values_part = jnp.einsum(
            "bqhk,bqhe->bkhe",
            weights.astype(jnp.bfloat16),
            grad_attended_heads,
            preferred_element_type=jnp.float32,
        )
        grad_weights = jnp.einsum(
            "bqhe,bkhe->bqhk", grad_attended_heads, value_part, preferred_element_type=jnp.float32
        )
        grad_scores = (weights * (grad_weights - row_delta[..., None]) * scale_factor).astype(
            jnp.bfloat16
        )
        grad_query = grad_query + jnp.einsum(
            "bqhk,bkhe->bqhe", grad_scores, key_part, preferred_element_type=jnp.float32
        )
        keys_part = jnp.einsum(
            "bqhk,bqhe->bkhe", grad_scores, query_heads, preferred_element_type=jnp.float32
        )
        grad_keys = lax.dynamic_update_slice_in_dim(grad_keys, keys_part, offset, 1)
        grad_values = lax.dynamic_update_slice_in_dim(grad_values, values_part, offset, 1)
        return ((grad_query, grad_keys, grad_values), None)

    zeros_keys = jnp.zeros((batch, key_rows, heads_here, HD), jnp.float32)
    back_init = (jnp.zeros((batch, tok_rows, heads_here, HD), jnp.float32), zeros_keys, zeros_keys)
    back_end, ignored = lax.scan(back_block, back_init, jnp.arange(block_count))
    grad_query_all, grad_keys_all, grad_values_all = back_end
    grad_keys_mine, grad_values_mine = (
        lax.psum_scatter(
            grad_keys_all.reshape(batch, key_rows, head_cols).astype(jnp.bfloat16),
            "ctx",
            scatter_dimension=1,
            tiled=True,
        ).astype(jnp.float32),
        lax.psum_scatter(
            grad_values_all.reshape(batch, key_rows, head_cols).astype(jnp.bfloat16),
            "ctx",
            scatter_dimension=1,
            tiled=True,
        ).astype(jnp.float32),
    )
    grad_query_flat = grad_query_all.reshape(batch, tok_rows, head_cols)
    grad_heads_bias = jnp.stack(
        [jnp.sum(grad_query_flat, axis=(0, 1)), jnp.sum(grad_values_mine, axis=(0, 1))]
    )
    grad_qkv_bf = jnp.stack([grad_query_flat, grad_keys_mine, grad_values_mine], axis=2).astype(
        jnp.bfloat16
    )
    grad_qkv_w = jnp.einsum(
        "btd,btcf->dcf", inputs, grad_qkv_bf, preferred_element_type=jnp.float32
    )
    input_part = jnp.einsum(
        "btcf,dcf->btd", grad_qkv_bf, qkv_full, preferred_element_type=jnp.float32
    )

    def fourth_rows(summed, row_start):
        return (grad_hidden_one + summed,)

    settled = settle(input_part, fourth_rows)
    grad_input = settled[0].astype(jnp.bfloat16)
    owned_grads = (
        lax.psum_scatter(
            grad_qkv_w.astype(jnp.bfloat16), ("weight", "ctx"), scatter_dimension=0, tiled=True
        ).astype(jnp.float32),
        lax.psum_scatter(
            grad_out_w.astype(jnp.bfloat16), ("weight", "ctx"), scatter_dimension=0, tiled=True
        ).astype(jnp.float32),
        lax.psum_scatter(
            grad_up_w.astype(jnp.bfloat16), ("weight", "ctx"), scatter_dimension=0, tiled=True
        ).astype(jnp.float32),
        lax.psum_scatter(
            grad_down_w.astype(jnp.bfloat16), ("weight", "ctx"), scatter_dimension=0, tiled=True
        ).astype(jnp.float32),
    )
    vector_sums = lax.psum(
        (
            grad_heads_bias,
            grad_up_b,
            jnp.stack([bias_out, bias_down]),
            jnp.stack([gain_one, gain_two]),
            jnp.stack([shift_one, shift_two]),
        ),
        ("weight", "ctx"),
    )
    return (
        layer_out,
        grad_input,
        owned_grads[0],
        owned_grads[1],
        owned_grads[2],
        owned_grads[3],
        vector_sums[0],
        vector_sums[1],
        vector_sums[2],
        vector_sums[3],
        vector_sums[4],
    )


def solution(mesh):
    return jax.shard_map(
        local,
        mesh=mesh,
        in_specs=(
            P("weight", "ctx", None),
            P("weight", None, "tensor"),
            P("weight", "tensor"),
            P("weight", "tensor"),
            P("weight", "tensor"),
            P(None, "tensor"),
            P("tensor"),
            P(),
            P(),
            P(),
            P("weight", "ctx", None),
        ),
        out_specs=(
            P("weight", "ctx", None),
            P("weight", "ctx", None),
            P(("weight", "ctx"), None, "tensor"),
            P(("weight", "ctx"), "tensor"),
            P(("weight", "ctx"), "tensor"),
            P(("weight", "ctx"), "tensor"),
            P(None, "tensor"),
            P("tensor"),
            P(),
            P(),
            P(),
        ),
        check_vma=False,
    )
```

profile of v0, /device:TPU:0, one launch (start us, length us, event | category | flops | bytes accessed | tf_op | source)
XLA Modules:
  0.0 652.9 jit_solution(9684503517704552660)
XLA Ops:
  7.3 2.4 copy.48
  9.8 10.0 %all_gather.23 = bf16[1024,256]{1,0:T(8,128)(2,1)} all-gather(bf16[512,256]{1,0:T(8,128)(2,1)S(1)} %copy-done.25), channel_id=1, replica_groups=mesh['weight'=2,'ctx'=4,'tensor'=4] {'weight'}, dimensions={0}, use_global_device_ids=true | all-gather | bytes 786432 | tf_op jit(solution)/shard_map/all_gather | solution.py:102
  19.8 19.8 %all-gather.5.cloned.1.call-done = bf16[1024,3,256]{0,2,1:T(8,128)(2,1)} async-done(((bf16[512,3,256]{0,2,1:T(8,128)(2,1)}), bf16[1024,3,256]{0,2,1:T(8,128)(2,1)}) %all-gather.5.cloned.1.call-update) | async-done | bytes 1572880 | tf_op jit(solution)/shard_map/all_gather | solution.py:101
  39.7 2.0 convolution_bitcast_fusion.5
  41.8 15.5 %all-gather = bf16[1,1024,1,256]{1,3,2,0:T(8,128)(2,1)S(1)} all-gather(bf16[1,256,1,256]{1,3,2,0:T(8,128)(2,1)S(1)} %slice.57), channel_id=2, replica_groups=mesh['weight'=2,'ctx'=4,'tensor'=4] {'ctx'}, dimensions={1}, use_global_device_ids=true | all-gather | bytes 655360 | tf_op jit(solution)/shard_map/all_gather | solution.py:119
  57.3 16.8 %all_gather.22 = bf16[1,1024,256]{1,2,0:T(8,128)(2,1)} all-gather(bf16[1,256,256]{1,2,0:T(8,128)(2,1)S(1)} %fusion.72), channel_id=1, replica_groups=mesh['weight'=2,'ctx'=4,'tensor'=4] {'ctx'}, dimensions={1}, use_global_device_ids=true | all-gather | bytes 655360 | tf_op jit(solution)/shard_map/all_gather | solution.py:120
  74.3 7.3 %while.30 = (s32[]{:T(128)}, f32[1,256,4,64]{1,3,2,0:T(8,128)S(1)}, f32[1,256,4]{1,2,0:T(4,128)S(1)}, f32[1,256,4]{1,2,0:T(4,128)S(1)}, s32[2]{0:T(128)S(1)}, /*...) while((s32[]{:T(128)}, f32[1,256,4,64]{1,3,2,0:T(8,128)S(1)}, ...), condition=%wide.region_3.4_spmd.clone, body=%wide.region_0.3_spmd.clone.sunk | while | flops 138614784 | bytes 7536843 | solution.py:79
  82.3 2.2 fusion.53
  86.0 32.2 %all-reduce.6.cloned.1.call-done = bf16[1,256,1024]{2,1,0:T(8,128)(2,1)} async-done(((bf16[1,256,1024]{2,1,0:T(8,128)(2,1)}), bf16[1,256,1024]{2,1,0:T(8,128)(2,1)}) %all-reduce.6.cloned.1.call-update) | async-done | bytes 524304 | tf_op jit(solution)/shard_map/psum | solution.py:44
  121.0 32.0 %all-gather.7.cloned.1.call-done = bf16[1024,1024]{1,0:T(8,128)(2,1)} async-done(((bf16[512,1024]{1,0:T(8,128)(2,1)}), bf16[1024,1024]{1,0:T(8,128)(2,1)}) %all-gather.7.cloned.1.call-update) | async-done | bytes 2097168 | tf_op jit(solution)/shard_map/all_gather | solution.py:103
  153.0 2.4 convolution_add_fusion
  155.5 32.1 %all-gather.9.cloned.1.call-done = bf16[1024,1024]{1,0:T(8,128)(2,1)} async-done(((bf16[512,1024]{1,0:T(8,128)(2,1)}), bf16[1024,1024]{1,0:T(8,128)(2,1)}) %all-gather.9.cloned.1.call-update) | async-done | bytes 2097168 | tf_op jit(solution)/shard_map/all_gather | solution.py:104
  187.6 3.1 fusion.51
  190.8 33.5 %all-reduce.8.cloned.1.call-done = bf16[1,256,1024]{2,1,0:T(8,128)(2,1)} async-done(((bf16[1,256,1024]{2,1,0:T(8,128)(2,1)}), bf16[1,256,1024]{2,1,0:T(8,128)(2,1)}) %all-reduce.8.cloned.1.call-update) | async-done | bytes 524304 | tf_op jit(solution)/shard_map/psum | solution.py:44
  231.9 33.4 %all-reduce.10.cloned.1.call-done = bf16[1,256,1024]{2,1,0:T(8,128)(2,1)} async-done(((bf16[1,256,1024]{2,1,0:T(8,128)(2,1)}), bf16[1,256,1024]{2,1,0:T(8,128)(2,1)}) %all-reduce.10.cloned.1.call-update) | async-done | bytes 524304 | tf_op jit(solution)/shard_map/psum | solution.py:44
  265.3 1.9 multiply_reduce_fusion
  270.9 15.2 %while.31 = (s32[]{:T(128)}, f32[1,256,4,64]{1,3,2,0:T(8,128)}, bf16[1,1024,4,64]{1,3,2,0:T(8,128)(2,1)}, bf16[1,1024,4,64]{1,3,2,0:T(8,128)(2,1)}, s32[2]{0:T(1...) while((s32[]{:T(128)}, f32[1,256,4,64]{1,3,2,0:T(8,128)}, ...), condition=%wide.region_17.18_spmd.clone, body=%wide.region_16.17_spmd.clone.sunk | while | flops 340393984 | bytes 22819192 | solution.py:228
  274.1 2.0 fusion.143
  281.6 2.1 fusion.143
  286.2 2.1 copy.50
  288.4 2.0 copy.49
  292.0 18.3 %reduce-scatter.11.cloned.1.call-done = bf16[1,256,256]{2,1,0:T(8,128)(2,1)} async-done(((bf16[1,1024,256]{2,1,0:T(8,128)(2,1)}), bf16[1,256,256]{2,1,0:T(8,128)(2,1)}) %reduce-scatter.11.cloned.1.call-update) | async-done | bytes 131088 | tf_op jit(solution)/shard_map/reduce_scatter | solution.py:237
  310.4 23.0 %reduce-scatter.9.cloned.1.call-done = bf16[1,256,256]{2,1,0:T(8,128)(2,1)} async-done(((bf16[1,1024,256]{2,1,0:T(8,128)(2,1)}), bf16[1,256,256]{2,1,0:T(8,128)(2,1)}) %reduce-scatter.9.cloned.1.call-update) | async-done | bytes 131088 | tf_op jit(solution)/shard_map/reduce_scatter | solution.py:231
  333.4 2.9 fusion.50
  336.4 3.4 convolution_convert_fusion.1
  339.9 3.3 convolution_convert_fusion
  347.4 50.3 %reduce-scatter.13.cloned.1.call-done = bf16[128,256]{1,0:T(8,128)(2,1)} async-done(((bf16[1024,256]{1,0:T(8,128)(2,1)}), bf16[128,256]{1,0:T(8,128)(2,1)}) %reduce-scatter.13.cloned.1.call-update) | async-done | bytes 65552 | tf_op jit(solution)/shard_map/reduce_scatter | solution.py:267
  399.3 35.9 %all-reduce = (f32[2,256]{1,0:T(2,128)}, f32[1024]{0:T(1024)}, f32[2,1024]{1,0:T(2,128)}, f32[2,1024]{1,0:T(2,128)}, f32[2,1024]{1,0:T(2,128)}) all-reduce(f32[2,256]{1,0:T(2,128)S(1)} %pad_maximum_fusion.6, f32[1024]{0:T(1024)S(1)} %get-tuple-element.288, ...), channel_id=1, replica_groups=mesh['weight'=2,'ctx'=4,'tensor'=4] {'weight','ctx'}, use_global_device_ids=true, to_apply=%region_27.28 | all-reduce | flops 7680 | bytes 61440 | tf_op jit(solution)/shard_map/psum | solution.py:277
  435.2 2.0 add_convert_fusion
  437.2 68.2 %reduce-scatter.15.cloned.1.call-done = bf16[128,1024]{1,0:T(8,128)(2,1)} async-done(((bf16[1024,1024]{1,0:T(8,128)(2,1)}), bf16[128,1024]{1,0:T(8,128)(2,1)}) %reduce-scatter.15.cloned.1.call-update) | async-done | bytes 262160 | tf_op jit(solution)/shard_map/reduce_scatter | solution.py:270
  507.2 69.1 %reduce-scatter.17.cloned.1.call-done = bf16[128,1024]{1,0:T(8,128)(2,1)} async-done(((bf16[1024,1024]{1,0:T(8,128)(2,1)}), bf16[128,1024]{1,0:T(8,128)(2,1)}) %reduce-scatter.17.cloned.1.call-update) | async-done | bytes 262160 | tf_op jit(solution)/shard_map/reduce_scatter | solution.py:273
  578.1 66.3 %reduce-scatter.19.cloned.1.call-done = bf16[128,768]{1,0:T(8,128)(2,1)} async-done(((bf16[1024,768]{1,0:T(8,128)(2,1)}), bf16[128,768]{1,0:T(8,128)(2,1)}) %reduce-scatter.19.cloned.1.call-update) | async-done | bytes 196624
  (184 shorter events, 45.1 us)
Async XLA Ops:
  7.2 32.5 %copy-start.2 = (bf16[1,256,1024]{2,1,0:T(8,128)(2,1)S(1)}, bf16[1,256,1024]{2,1,0:T(8,128)(2,1)}, u32[]{:S(2)}) copy-start(bf16[1,256,1024]{2,1,0:T(8,128)(2,1)} %param.15) | copy-start | bytes 1572868
  7.2 32.5 %all-gather.5.cloned.1.call-start = ((), (), s32[]{:S(2)}) async-start(), calls=%async_computation.6 | async-start | bytes 2359296 | tf_op jit(solution)/shard_map/all_gather | solution.py:101
  9.6 108.6 %all-reduce.6.cloned.1.call-start = ((), (), s32[]{:S(2)}) async-start(), calls=%async_computation.7 | async-start | bytes 1048576 | tf_op jit(solution)/shard_map/psum | solution.py:44
  81.6 4.3 copy-start.12
  81.6 4.3 copy-start.27
  81.6 4.3 copy-start.28
  81.6 4.4 copy-start.29
  84.6 68.5 %copy-start.33 = (f32[1024]{0:T(1024)S(1)}, f32[1024]{0:T(1024)}, u32[]{:S(2)}) copy-start(f32[1024]{0:T(1024)} %param.21) | copy-start | bytes 12292
  84.6 68.5 %all-gather.7.cloned.1.call-start = ((), (), s32[]{:S(2)}) async-start(), calls=%async_computation.8 | async-start | bytes 3145728 | tf_op jit(solution)/shard_map/all_gather | solution.py:103
  85.3 102.3 %all-gather.9.cloned.1.call-start = ((), (), s32[]{:S(2)}) async-start(), calls=%async_computation.9 | async-start | bytes 3145728 | tf_op jit(solution)/shard_map/all_gather | solution.py:104
  85.9 138.4 %all-reduce.8.cloned.1.call-start = ((), (), s32[]{:S(2)}) async-start(), calls=%async_computation.10 | async-start | bytes 1048576 | tf_op jit(solution)/shard_map/psum | solution.py:44
  118.3 34.8 %copy-start.9 = (bf16[1,256,1024]{2,1,0:T(8,128)(2,1)S(1)}, bf16[1,256,1024]{2,1,0:T(8,128)(2,1)}, u32[]{:S(2)}) copy-start(bf16[1,256,1024]{2,1,0:T(8,128)(2,1)} %all-reduce.6.cloned.1.call-done) | copy-start | bytes 1572868
  155.5 35.2 %copy-start.23 = (f32[256,1024]{1,0:T(8,128)}, f32[256,1024]{1,0:T(8,128)S(1)}, u32[]{:S(2)}) copy-start(f32[256,1024]{1,0:T(8,128)S(1)} %convolution_add_fusion) | copy-start | bytes 3145732
  190.7 35.5 %copy-start.17 = (bf16[1,256,1024]{2,1,0:T(8,128)(2,1)S(1)}, bf16[1,256,1024]{2,1,0:T(8,128)(2,1)}, u32[]{:S(2)}) copy-start(bf16[1,256,1024]{2,1,0:T(8,128)(2,1)} %param.25) | copy-start | bytes 1572868
  190.7 74.6 %all-reduce.10.cloned.1.call-start = ((), (), s32[]{:S(2)}) async-start(), calls=%async_computation.11 | async-start | bytes 1048576 | tf_op jit(solution)/shard_map/psum | solution.py:44
  228.0 39.2 %copy-start.7 = (f32[1,256,1024]{2,1,0:T(8,128)}, f32[1,256,1024]{2,1,0:T(8,128)S(1)}, u32[]{:S(2)}) copy-start(f32[1,256,1024]{2,1,0:T(8,128)S(1)} %get-tuple-element.276) | copy-start | bytes 3145732
  229.2 38.0 %copy-start.34 = (bf16[256,1024]{1,0:T(8,128)(2,1)}, bf16[256,1024]{1,0:T(8,128)(2,1)S(1)}, u32[]{:S(2)}) copy-start(bf16[256,1024]{1,0:T(8,128)(2,1)S(1)} %get-tuple-element.289) | copy-start | bytes 1572868
  229.2 36.1 %copy-start.10 = (bf16[1,256,1024]{2,1,0:T(8,128)(2,1)S(1)}, bf16[1,256,1024]{2,1,0:T(8,128)(2,1)}, u32[]{:S(2)}) copy-start(bf16[1,256,1024]{2,1,0:T(8,128)(2,1)} %all-reduce.6.cloned.1.call-done) | copy-start | bytes 1572868
  231.7 78.7 %reduce-scatter.11.cloned.1.call-start = ((), (), s32[]{:S(2)}) async-start(), calls=%async_computation.13 | async-start | bytes 655360 | tf_op jit(solution)/shard_map/reduce_scatter | solution.py:237
  281.6 3.3 copy-start.19
  286.2 4.3 copy-start.6
  286.2 4.3 copy-start.22
  288.3 3.5 copy-start.14
  288.3 45.1 %reduce-scatter.9.cloned.1.call-start = ((), (), s32[]{:S(2)}) async-start(), calls=%async_computation.12 | async-start | bytes 655360 | tf_op jit(solution)/shard_map/reduce_scatter | solution.py:231
  290.4 107.3 %reduce-scatter.13.cloned.1.call-start = ((), (), s32[]{:S(2)}) async-start(), calls=%async_computation.15 | async-start | bytes 589824 | tf_op jit(solution)/shard_map/reduce_scatter | solution.py:267
  291.7 143.5 %all-reduce.12.cloned.1.call-start = ((), (), s32[]{:S(2)}) async-start(), calls=%async_computation.14 | async-start | bytes 1048576 | tf_op jit(solution)/shard_map/psum | solution.py:44
  291.8 44.6 %copy-start.3 = (bf16[1,256,1024]{2,1,0:T(8,128)(2,1)S(1)}, bf16[1,256,1024]{2,1,0:T(8,128)(2,1)}, u32[]{:S(2)}) copy-start(bf16[1,256,1024]{2,1,0:T(8,128)(2,1)} %param.15) | copy-start | bytes 1572868
  291.8 44.6 %copy-start.11 = (bf16[1,256,1024]{2,1,0:T(8,128)(2,1)S(1)}, bf16[1,256,1024]{2,1,0:T(8,128)(2,1)}, u32[]{:S(2)}) copy-start(bf16[1,256,1024]{2,1,0:T(8,128)(2,1)} %all-reduce.6.cloned.1.call-done) | copy-start | bytes 1572868
  336.3 3.5 copy-start.8
  336.3 169.1 %reduce-scatter.15.cloned.1.call-start = ((), (), s32[]{:S(2)}) async-start(), calls=%async_computation.16 | async-start | bytes 2359296 | tf_op jit(solution)/shard_map/reduce_scatter | solution.py:270
  339.8 236.5 %reduce-scatter.17.cloned.1.call-start = ((), (), s32[]{:S(2)}) async-start(), calls=%async_computation.17 | async-start | bytes 2359296 | tf_op jit(solution)/shard_map/reduce_scatter | solution.py:273
  343.2 301.1 %reduce-scatter.19.cloned.1.call-start = ((), (), s32[]{:S(2)}) async-start(), calls=%async_computation.18 | async-start | bytes 1769472
  (21 other events, 34.4 us)
Sparse Core Ops, SparseCore 0:
  9.8 29.8 all-gather.4
  84.7 33.5 all-reduce.5
  119.8 33.1 all-gather.6
  154.4 33.0 all-gather.8
  190.8 33.4 all-reduce.7
  231.8 33.5 all-reduce.9
  288.4 21.8 reduce-scatter.10
  313.2 20.1 reduce-scatter.8
  336.7 60.9 reduce-scatter.12
  400.5 32.4 all-reduce.11
  436.5 68.8 reduce-scatter.14
  508.8 67.4 reduce-scatter.16
  579.7 64.6 reduce-scatter.18
where the time goes:
time: 654 us; the launch traced here: 653 us
  waiting for transfers between devices  480 us (73%)
  blocking collectives  78.3 us (12%)
  matrix products  38.7 us (6%)
  local copies, waits for them, and re-layouts  20.9 us (3%)
  other arithmetic  17.2 us (3%)
  between operations  14.5 us (2%)
    psum x4, waiting for transfers between devices, settle(): lax.psum(partial_value.astype(jnp.bfloat16), 'tensor').astype(jnp.float32)  99.2 us
    reduce_scatter x1, waiting for transfers between devices, local(): lax.psum_scatter(grad_down_w.astype(jnp.bfloat16), ('weight', 'ctx'), sca...  69.1 us
    reduce_scatter x1, waiting for transfers between devices, local(): lax.psum_scatter(grad_up_w.astype(jnp.bfloat16), ('weight', 'ctx'), scatt...  68.2 us
    unnamed x14, waiting for transfers between devices  67.7 us
    reduce_scatter x1, waiting for transfers between devices, local(): lax.psum_scatter(grad_out_w.astype(jnp.bfloat16), ('weight', 'ctx'), scat...  50.3 us
    psum x1, blocking collectives, local(): lax.psum((grad_heads_bias, grad_up_b, jnp.stack([bias_out, bias_down]), j...  35.9 us
    all_gather x1, waiting for transfers between devices, local(): lax.all_gather(w_down, 'weight', axis=0, tiled=True)  32.1 us
    all_gather x1, waiting for transfers between devices, local(): lax.all_gather(w_up, 'weight', axis=0, tiled=True)  32 us
  transfers between devices with their start and end apart: 13, of which 12 were waited for; matrix products, arithmetic and copies ran while one was open for 4% of the time, Pallas kernels for 0%

commit v1 on v0

--- a/solution.py
+++ b/solution.py
@@ -274,16 +274,15 @@
             grad_down_w.astype(jnp.bfloat16), ("weight", "ctx"), scatter_dimension=0, tiled=True
         ).astype(jnp.float32),
     )
-    vector_sums = lax.psum(
-        (
-            grad_heads_bias,
-            grad_up_b,
-            jnp.stack([bias_out, bias_down]),
-            jnp.stack([gain_one, gain_two]),
-            jnp.stack([shift_one, shift_two]),
-        ),
-        ("weight", "ctx"),
-    )
+    vector_sums = (
+        grad_heads_bias,
+        grad_up_b,
+        jnp.stack([bias_out, bias_down]),
+        jnp.stack([gain_one, gain_two]),
+        jnp.stack([shift_one, shift_two]),
+    )
+    for name in ("weight", "ctx"):
+        vector_sums = lax.psum(vector_sums, name)
     return (
         layer_out,
         grad_input,

time: 654 us -> 654 us (level)
  blocking collectives: 78.3 us -> 68.2 us
  waiting for transfers between devices: 480 us -> 490 us
    psum x1 -> x2, blocking collectives: 35.9 us -> 25.9 us  [local(): vector_sums = lax.psum(vector_sums, name)]
    psum x4, waiting for transfers between devices: 99.2 us -> 107 us  [settle(): lax.psum(partial_value.astype(jnp.bfloat16), 'tensor').astype(jnp.float32)]
  transfers between devices with their start and end apart: 13 -> 13, of which waited for: 12 -> 13; matrix products, arithmetic and copies ran while one was open for 4% -> 4% of each run, Pallas kernels for 0% -> 0%
where the time goes in v1:
time: 654 us; the launch traced here: 653 us
  waiting for transfers between devices  490 us (75%)
  blocking collectives  68.2 us (10%)
  matrix products  38.7 us (6%)
  local copies, waits for them, and re-layouts  20.9 us (3%)
  other arithmetic  17.2 us (3%)
  between operations  14.5 us (2%)
    psum x4, waiting for transfers between devices, settle(): lax.psum(partial_value.astype(jnp.bfloat16), 'tensor').astype(jnp.float32)  107 us
    reduce_scatter x1, waiting for transfers between devices, local(): lax.psum_scatter(grad_up_w.astype(jnp.bfloat16), ('weight', 'ctx'), scatt...  70.5 us
    reduce_scatter x1, waiting for transfers between devices, local(): lax.psum_scatter(grad_down_w.astype(jnp.bfloat16), ('weight', 'ctx'), sca...  69.1 us
    unnamed x14, waiting for transfers between devices  67.8 us
    reduce_scatter x1, waiting for transfers between devices, local(): lax.psum_scatter(grad_out_w.astype(jnp.bfloat16), ('weight', 'ctx'), scat...  50.3 us
    all_gather x1, waiting for transfers between devices, local(): lax.all_gather(w_down, 'weight', axis=0, tiled=True)  32.1 us
    all_gather x1, waiting for transfers between devices, local(): lax.all_gather(w_up, 'weight', axis=0, tiled=True)  32 us
    psum x2, blocking collectives, local(): vector_sums = lax.psum(vector_sums, name)  25.9 us
  transfers between devices with their start and end apart: 13, of which 13 were waited for; matrix products, arithmetic and copies ran while one was open for 4% of the time, Pallas kernels for 0%

profile of v1, /device:TPU:0, one launch (start us, length us, event | category | flops | bytes accessed | tf_op | source)
XLA Modules:
  0.0 653.0 jit_solution(13501467801954487957)
XLA Ops:
  7.3 2.4 copy.48
  9.8 10.0 %all_gather.23 = bf16[1024,256]{1,0:T(8,128)(2,1)} all-gather(bf16[512,256]{1,0:T(8,128)(2,1)S(1)} %copy-done.25), channel_id=1, replica_groups=mesh['weight'=2,'ctx'=4,'tensor'=4] {'weight'}, dimensions={0}, use_global_device_ids=true | all-gather | bytes 786432 | tf_op jit(solution)/shard_map/all_gather | solution.py:102
  19.8 19.8 %all-gather.5.cloned.1.call-done = bf16[1024,3,256]{0,2,1:T(8,128)(2,1)} async-done(((bf16[512,3,256]{0,2,1:T(8,128)(2,1)}), bf16[1024,3,256]{0,2,1:T(8,128)(2,1)}) %all-gather.5.cloned.1.call-update) | async-done | bytes 1572880 | tf_op jit(solution)/shard_map/all_gather | solution.py:101
  39.7 2.0 convolution_bitcast_fusion.5
  41.8 15.5 %all-gather = bf16[1,1024,1,256]{1,3,2,0:T(8,128)(2,1)S(1)} all-gather(bf16[1,256,1,256]{1,3,2,0:T(8,128)(2,1)S(1)} %slice.57), channel_id=2, replica_groups=mesh['weight'=2,'ctx'=4,'tensor'=4] {'ctx'}, dimensions={1}, use_global_device_ids=true | all-gather | bytes 655360 | tf_op jit(solution)/shard_map/all_gather | solution.py:119
  57.3 16.8 %all_gather.22 = bf16[1,1024,256]{1,2,0:T(8,128)(2,1)} all-gather(bf16[1,256,256]{1,2,0:T(8,128)(2,1)S(1)} %fusion.72), channel_id=1, replica_groups=mesh['weight'=2,'ctx'=4,'tensor'=4] {'ctx'}, dimensions={1}, use_global_device_ids=true | all-gather | bytes 655360 | tf_op jit(solution)/shard_map/all_gather | solution.py:120
  74.3 7.3 %while.30 = (s32[]{:T(128)}, f32[1,256,4,64]{1,3,2,0:T(8,128)S(1)}, f32[1,256,4]{1,2,0:T(4,128)S(1)}, f32[1,256,4]{1,2,0:T(4,128)S(1)}, s32[2]{0:T(128)S(1)}, /*...) while((s32[]{:T(128)}, f32[1,256,4,64]{1,3,2,0:T(8,128)S(1)}, ...), condition=%wide.region_3.4_spmd.clone, body=%wide.region_0.3_spmd.clone.sunk | while | flops 138614784 | bytes 7536843 | solution.py:79
  82.3 2.2 fusion.53
  86.0 32.2 %all-reduce.7.cloned.1.call-done = bf16[1,256,1024]{2,1,0:T(8,128)(2,1)} async-done(((bf16[1,256,1024]{2,1,0:T(8,128)(2,1)}), bf16[1,256,1024]{2,1,0:T(8,128)(2,1)}) %all-reduce.7.cloned.1.call-update) | async-done | bytes 524304 | tf_op jit(solution)/shard_map/psum | solution.py:44
  121.0 32.0 %all-gather.7.cloned.1.call-done = bf16[1024,1024]{1,0:T(8,128)(2,1)} async-done(((bf16[512,1024]{1,0:T(8,128)(2,1)}), bf16[1024,1024]{1,0:T(8,128)(2,1)}) %all-gather.7.cloned.1.call-update) | async-done | bytes 2097168 | tf_op jit(solution)/shard_map/all_gather | solution.py:103
  153.0 2.4 convolution_add_fusion
  155.5 32.1 %all-gather.9.cloned.1.call-done = bf16[1024,1024]{1,0:T(8,128)(2,1)} async-done(((bf16[512,1024]{1,0:T(8,128)(2,1)}), bf16[1024,1024]{1,0:T(8,128)(2,1)}) %all-gather.9.cloned.1.call-update) | async-done | bytes 2097168 | tf_op jit(solution)/shard_map/all_gather | solution.py:104
  187.6 3.1 fusion.51
  190.8 33.5 %all-reduce.9.cloned.1.call-done = bf16[1,256,1024]{2,1,0:T(8,128)(2,1)} async-done(((bf16[1,256,1024]{2,1,0:T(8,128)(2,1)}), bf16[1,256,1024]{2,1,0:T(8,128)(2,1)}) %all-reduce.9.cloned.1.call-update) | async-done | bytes 524304 | tf_op jit(solution)/shard_map/psum | solution.py:44
  231.9 33.4 %all-reduce.11.cloned.1.call-done = bf16[1,256,1024]{2,1,0:T(8,128)(2,1)} async-done(((bf16[1,256,1024]{2,1,0:T(8,128)(2,1)}), bf16[1,256,1024]{2,1,0:T(8,128)(2,1)}) %all-reduce.11.cloned.1.call-update) | async-done | bytes 524304 | tf_op jit(solution)/shard_map/psum | solution.py:44
  270.9 15.2 %while.31 = (s32[]{:T(128)}, f32[1,256,4,64]{1,3,2,0:T(8,128)}, bf16[1,1024,4,64]{1,3,2,0:T(8,128)(2,1)}, bf16[1,1024,4,64]{1,3,2,0:T(8,128)(2,1)}, s32[2]{0:T(1...) while((s32[]{:T(128)}, f32[1,256,4,64]{1,3,2,0:T(8,128)}, ...), condition=%wide.region_17.18_spmd.clone, body=%wide.region_16.17_spmd.clone.sunk | while | flops 340393984 | bytes 22819192 | solution.py:228
  274.1 2.0 fusion.143
  281.6 2.1 fusion.143
  286.2 2.1 copy.50
  288.4 2.0 copy.49
  292.0 18.3 %reduce-scatter.11.cloned.1.call-done = bf16[1,256,256]{2,1,0:T(8,128)(2,1)} async-done(((bf16[1,1024,256]{2,1,0:T(8,128)(2,1)}), bf16[1,256,256]{2,1,0:T(8,128)(2,1)}) %reduce-scatter.11.cloned.1.call-update) | async-done | bytes 131088 | tf_op jit(solution)/shard_map/reduce_scatter | solution.py:237
  310.4 23.0 %reduce-scatter.9.cloned.1.call-done = bf16[1,256,256]{2,1,0:T(8,128)(2,1)} async-done(((bf16[1,1024,256]{2,1,0:T(8,128)(2,1)}), bf16[1,256,256]{2,1,0:T(8,128)(2,1)}) %reduce-scatter.9.cloned.1.call-update) | async-done | bytes 131088 | tf_op jit(solution)/shard_map/reduce_scatter | solution.py:231
  333.4 2.9 fusion.50
  336.4 3.4 convolution_convert_fusion.1
  339.9 3.3 convolution_convert_fusion
  347.4 50.3 %reduce-scatter.13.cloned.1.call-done = bf16[128,256]{1,0:T(8,128)(2,1)} async-done(((bf16[1024,256]{1,0:T(8,128)(2,1)}), bf16[128,256]{1,0:T(8,128)(2,1)}) %reduce-scatter.13.cloned.1.call-update) | async-done | bytes 65552 | tf_op jit(solution)/shard_map/reduce_scatter | solution.py:267
  399.3 8.2 %all-reduce.1 = (f32[2,256]{1,0:T(2,128)S(1)}, f32[1024]{0:T(1024)S(1)}, f32[2,1024]{1,0:T(2,128)S(1)}, f32[2,1024]{1,0:T(2,128)S(1)}, f32[2,1024]{1,0:T(2,128)S(1)}) all-reduce(f32[2,256]{1,0:T(2,128)S(1)} %pad_maximum_fusion.6, f32[1024]{0:T(1024)S(1)} %get-tuple-element.293, ...), channel_id=1, replica_groups=mesh['weight'=2,'ctx'=4,'tensor'=4] {'weight'}, use_global_device_ids=true, to_apply=%region_27.28 | all-reduce | flops 7680 | bytes 61440 | tf_op jit(solution)/shard_map/psum | solution.py:285
  407.4 17.8 %all-reduce = (f32[2,256]{1,0:T(2,128)}, f32[1024]{0:T(1024)}, f32[2,1024]{1,0:T(2,128)}, f32[2,1024]{1,0:T(2,128)}, f32[2,1024]{1,0:T(2,128)}) all-reduce(f32[2,256]{1,0:T(2,128)S(1)} %get-tuple-element.268, f32[1024]{0:T(1024)S(1)} %get-tuple-element.269, ...), channel_id=1, replica_groups=mesh['weight'=2,'ctx'=4,'tensor'=4] {'ctx'}, use_global_device_ids=true, to_apply=%region_28.29 | all-reduce | flops 7680 | bytes 61440 | tf_op jit(solution)/shard_map/psum | solution.py:285
  425.2 7.7 %all-reduce.13.cloned.1.call-done = bf16[1,256,1024]{2,1,0:T(8,128)(2,1)} async-done(((bf16[1,256,1024]{2,1,0:T(8,128)(2,1)}), bf16[1,256,1024]{2,1,0:T(8,128)(2,1)}) %all-reduce.13.cloned.1.call-update) | async-done | bytes 524304 | tf_op jit(solution)/shard_map/psum | solution.py:44
  434.9 70.5 %reduce-scatter.15.cloned.1.call-done = bf16[128,1024]{1,0:T(8,128)(2,1)} async-done(((bf16[1024,1024]{1,0:T(8,128)(2,1)}), bf16[128,1024]{1,0:T(8,128)(2,1)}) %reduce-scatter.15.cloned.1.call-update) | async-done | bytes 262160 | tf_op jit(solution)/shard_map/reduce_scatter | solution.py:270
  507.2 69.1 %reduce-scatter.17.cloned.1.call-done = bf16[128,1024]{1,0:T(8,128)(2,1)} async-done(((bf16[1024,1024]{1,0:T(8,128)(2,1)}), bf16[128,1024]{1,0:T(8,128)(2,1)}) %reduce-scatter.17.cloned.1.call-update) | async-done | bytes 262160 | tf_op jit(solution)/shard_map/reduce_scatter | solution.py:273
  578.1 66.4 %reduce-scatter.19.cloned.1.call-done = bf16[128,768]{1,0:T(8,128)(2,1)} async-done(((bf16[1024,768]{1,0:T(8,128)(2,1)}), bf16[128,768]{1,0:T(8,128)(2,1)}) %reduce-scatter.19.cloned.1.call-update) | async-done | bytes 196624
  (185 shorter events, 49.0 us)
Async XLA Ops:
  7.2 32.5 %copy-start.2 = (bf16[1,256,1024]{2,1,0:T(8,128)(2,1)S(1)}, bf16[1,256,1024]{2,1,0:T(8,128)(2,1)}, u32[]{:S(2)}) copy-start(bf16[1,256,1024]{2,1,0:T(8,128)(2,1)} %param.15) | copy-start | bytes 1572868
  7.2 32.5 %all-gather.5.cloned.1.call-start = ((), (), s32[]{:S(2)}) async-start(), calls=%async_computation.6 | async-start | bytes 2359296 | tf_op jit(solution)/shard_map/all_gather | solution.py:101
  9.6 108.6 %all-reduce.7.cloned.1.call-start = ((), (), s32[]{:S(2)}) async-start(), calls=%async_computation.7 | async-start | bytes 1048576 | tf_op jit(solution)/shard_map/psum | solution.py:44
  81.6 4.3 copy-start.12
  81.6 4.3 copy-start.27
  81.6 4.3 copy-start.28
  81.6 4.4 copy-start.29
  84.6 68.5 %copy-start.33 = (f32[1024]{0:T(1024)S(1)}, f32[1024]{0:T(1024)}, u32[]{:S(2)}) copy-start(f32[1024]{0:T(1024)} %param.21) | copy-start | bytes 12292
  84.6 68.5 %all-gather.7.cloned.1.call-start = ((), (), s32[]{:S(2)}) async-start(), calls=%async_computation.8 | async-start | bytes 3145728 | tf_op jit(solution)/shard_map/all_gather | solution.py:103
  85.3 102.3 %all-gather.9.cloned.1.call-start = ((), (), s32[]{:S(2)}) async-start(), calls=%async_computation.9 | async-start | bytes 3145728 | tf_op jit(solution)/shard_map/all_gather | solution.py:104
  85.9 138.4 %all-reduce.9.cloned.1.call-start = ((), (), s32[]{:S(2)}) async-start(), calls=%async_computation.10 | async-start | bytes 1048576 | tf_op jit(solution)/shard_map/psum | solution.py:44
  118.3 34.8 %copy-start.9 = (bf16[1,256,1024]{2,1,0:T(8,128)(2,1)S(1)}, bf16[1,256,1024]{2,1,0:T(8,128)(2,1)}, u32[]{:S(2)}) copy-start(bf16[1,256,1024]{2,1,0:T(8,128)(2,1)} %all-reduce.7.cloned.1.call-done) | copy-start | bytes 1572868
  155.5 35.2 %copy-start.23 = (f32[256,1024]{1,0:T(8,128)}, f32[256,1024]{1,0:T(8,128)S(1)}, u32[]{:S(2)}) copy-start(f32[256,1024]{1,0:T(8,128)S(1)} %convolution_add_fusion) | copy-start | bytes 3145732
  190.7 35.5 %copy-start.17 = (bf16[1,256,1024]{2,1,0:T(8,128)(2,1)S(1)}, bf16[1,256,1024]{2,1,0:T(8,128)(2,1)}, u32[]{:S(2)}) copy-start(bf16[1,256,1024]{2,1,0:T(8,128)(2,1)} %param.25) | copy-start | bytes 1572868
  190.7 74.6 %all-reduce.11.cloned.1.call-start = ((), (), s32[]{:S(2)}) async-start(), calls=%async_computation.11 | async-start | bytes 1048576 | tf_op jit(solution)/shard_map/psum | solution.py:44
  228.0 39.2 %copy-start.7 = (f32[1,256,1024]{2,1,0:T(8,128)}, f32[1,256,1024]{2,1,0:T(8,128)S(1)}, u32[]{:S(2)}) copy-start(f32[1,256,1024]{2,1,0:T(8,128)S(1)} %get-tuple-element.281) | copy-start | bytes 3145732
  229.2 38.0 %copy-start.34 = (bf16[256,1024]{1,0:T(8,128)(2,1)}, bf16[256,1024]{1,0:T(8,128)(2,1)S(1)}, u32[]{:S(2)}) copy-start(bf16[256,1024]{1,0:T(8,128)(2,1)S(1)} %get-tuple-element.294) | copy-start | bytes 1572868
  229.2 36.1 %copy-start.10 = (bf16[1,256,1024]{2,1,0:T(8,128)(2,1)S(1)}, bf16[1,256,1024]{2,1,0:T(8,128)(2,1)}, u32[]{:S(2)}) copy-start(bf16[1,256,1024]{2,1,0:T(8,128)(2,1)} %all-reduce.7.cloned.1.call-done) | copy-start | bytes 1572868
  231.7 78.7 %reduce-scatter.11.cloned.1.call-start = ((), (), s32[]{:S(2)}) async-start(), calls=%async_computation.13 | async-start | bytes 655360 | tf_op jit(solution)/shard_map/reduce_scatter | solution.py:237
  281.6 3.3 copy-start.19
  286.2 4.3 copy-start.6
  286.2 4.3 copy-start.22
  288.3 3.5 copy-start.14
  288.3 45.1 %reduce-scatter.9.cloned.1.call-start = ((), (), s32[]{:S(2)}) async-start(), calls=%async_computation.12 | async-start | bytes 655360 | tf_op jit(solution)/shard_map/reduce_scatter | solution.py:231
  290.4 107.3 %reduce-scatter.13.cloned.1.call-start = ((), (), s32[]{:S(2)}) async-start(), calls=%async_computation.15 | async-start | bytes 589824 | tf_op jit(solution)/shard_map/reduce_scatter | solution.py:267
  291.7 141.2 %all-reduce.13.cloned.1.call-start = ((), (), s32[]{:S(2)}) async-start(), calls=%async_computation.14 | async-start | bytes 1048576 | tf_op jit(solution)/shard_map/psum | solution.py:44
  291.8 44.6 %copy-start.3 = (bf16[1,256,1024]{2,1,0:T(8,128)(2,1)S(1)}, bf16[1,256,1024]{2,1,0:T(8,128)(2,1)}, u32[]{:S(2)}) copy-start(bf16[1,256,1024]{2,1,0:T(8,128)(2,1)} %param.15) | copy-start | bytes 1572868
  291.8 44.6 %copy-start.11 = (bf16[1,256,1024]{2,1,0:T(8,128)(2,1)S(1)}, bf16[1,256,1024]{2,1,0:T(8,128)(2,1)}, u32[]{:S(2)}) copy-start(bf16[1,256,1024]{2,1,0:T(8,128)(2,1)} %all-reduce.7.cloned.1.call-done) | copy-start | bytes 1572868
  336.3 3.5 copy-start.8
  336.3 169.1 %reduce-scatter.15.cloned.1.call-start = ((), (), s32[]{:S(2)}) async-start(), calls=%async_computation.16 | async-start | bytes 2359296 | tf_op jit(solution)/shard_map/reduce_scatter | solution.py:270
  339.8 236.5 %reduce-scatter.17.cloned.1.call-start = ((), (), s32[]{:S(2)}) async-start(), calls=%async_computation.17 | async-start | bytes 2359296 | tf_op jit(solution)/shard_map/reduce_scatter | solution.py:273
  343.2 301.3 %reduce-scatter.19.cloned.1.call-start = ((), (), s32[]{:S(2)}) async-start(), calls=%async_computation.18 | async-start | bytes 1769472
  (21 other events, 34.4 us)
Sparse Core Ops, SparseCore 0:
  9.8 29.8 all-gather.4
  84.7 33.5 all-reduce.6
  119.8 33.1 all-gather.6
  154.4 33.0 all-gather.8
  190.8 33.4 all-reduce.8
  231.8 33.5 all-reduce.10
  288.4 21.8 reduce-scatter.10
  313.2 20.1 reduce-scatter.8
  336.7 60.9 reduce-scatter.12
  400.5 32.4 all-reduce.12
  436.5 68.8 reduce-scatter.14
  508.8 67.4 reduce-scatter.16
  579.7 64.7 reduce-scatter.18
